TPU v7x, 32 devices: a whole 2x2x4 slice. The times are simulated.
32 devices in a mesh: group: 4 (over y, x), seq: 8 (over z, core).
Axes of the slice: x: 2, y: 2, z: 4, core: 2. Of those that a mesh axis runs over, the one named last changes fastest.
Arguments:
- tokens: bfloat16 [32, 2048, 2048], P('group', 'seq'), may hold values from -6 to 6
- image_keys: bfloat16 [32, 256, 2048], P('group', 'seq'), may hold values from -256 to 256
- image_values: bfloat16 [32, 256, 2048], P('group', 'seq'), may hold values from -18 to 18
- text_len: int32 [32], replicated, may hold values from 1 to 2048
- image_len: int32 [32], replicated, may hold values from 1 to 256
- counts: int32 [6], replicated, may hold values from 1 to 4, as said below
- old_group: int32 [6], replicated, may hold values from 0 to 3, as said below
- new_group: int32 [6], replicated, may hold values from 0 to 3, as said below
- w_query: bfloat16 [2048, 2048], replicated, may hold values from -0.125 to 0.125
- w_out: bfloat16 [2048, 2048], replicated, may hold values from -0.125 to 0.125
Outputs:
- layer_out: bfloat16 [32, 2048, 2048], P('group', 'seq')
Inputs may be any that keep to these rules, and one draw needn't show every extreme that they name: `counts`: every task has at most 4 samples, and some task has exactly 4. `old_group`: each group is the old group of at most two tasks, and no two tasks share both their old group and their new group, so at most 4 samples go from one old group to one new group. `new_group`: each group is the new group of at most two tasks.
All inputs are finite; a program needn't handle non-finite values.
Results may differ from a plain program's by a relative error of at most 0.011.
Values may be sent and summed in bfloat16 or wider, within the bound.
A program may use at most 128 MiB of HBM per device.

v0:
```python
import jax
import jax.numpy as jnp
from jax import lax
from jax.sharding import PartitionSpec as P

HEAD_DIM = 128
HALF = 4
masked_score = -1e30
norm_eps = 1e-05


def layout(counts, old_group, new_group, group_count, slot_count):
    task_order = jnp.arange(counts.shape[0], dtype=jnp.int32)
    earlier = task_order[None, :] < task_order[:, None]
    same_old = old_group[None, :] == old_group[:, None]
    same_new = new_group[None, :] == new_group[:, None]
    old_start = jnp.sum(jnp.where(earlier & same_old, counts[None, :], 0), axis=1)
    new_start = jnp.sum(jnp.where(earlier & same_new, counts[None, :], 0), axis=1)
    target = jnp.arange(group_count * slot_count, dtype=jnp.int32)
    target_group = target // slot_count
    target_slot = target % slot_count
    matches = (
        (new_group[None, :] == target_group[:, None])
        & (target_slot[:, None] >= new_start[None, :])
        & (target_slot[:, None] < (new_start + counts)[None, :])
    )
    filled = jnp.any(matches, axis=1)
    offset = target_slot - jnp.sum(jnp.where(matches, new_start[None, :], 0), axis=1)
    source_group = jnp.sum(jnp.where(matches, old_group[None, :], 0), axis=1)
    source_slot = jnp.sum(jnp.where(matches, old_start[None, :], 0), axis=1) + offset
    return (filled, source_group, source_slot, offset, old_start)


def normalize(samples_rows):
    values = samples_rows.astype(jnp.float32)
    average = jnp.mean(values, axis=-1, keepdims=True)
    centred = values - average
    variance = jnp.mean(centred * centred, axis=-1, keepdims=True)
    return (centred * lax.rsqrt(variance + norm_eps)).astype(jnp.bfloat16)


def spread_rows(source_array, source_index, wanted):
    gathered = jnp.take(source_array, source_index, axis=0)
    return jnp.where(wanted[:, None, None], gathered, jnp.zeros((), source_array.dtype))


def regroup(joined, group_index, group_count, slot_count, tables, counts, old_group, new_group):
    filled, source_group, source_slot, offset, old_start = tables
    own_first = group_index * slot_count
    filled_here = lax.dynamic_slice_in_dim(filled, own_first, slot_count)
    from_group = lax.dynamic_slice_in_dim(source_group, own_first, slot_count)
    destinations = jnp.arange(group_count, dtype=jnp.int32)
    pairing = (old_group[None, :] == group_index) & (new_group[None, :] == destinations[:, None])
    pair_first = jnp.sum(jnp.where(pairing, old_start[None, :], 0), axis=1)
    pair_amount = jnp.sum(jnp.where(pairing, counts[None, :], 0), axis=1)
    position = jnp.arange(HALF, dtype=jnp.int32)
    sending = (position[None, :] < pair_amount[:, None]).reshape(-1)
    source_index = jnp.where(sending, (pair_first[:, None] + position[None, :]).reshape(-1), 0)
    outgoing = spread_rows(joined, source_index, sending)
    incoming = lax.all_to_all(outgoing, "group", split_axis=0, concat_axis=0, tiled=True)
    chosen = from_group * HALF + lax.dynamic_slice_in_dim(offset, own_first, slot_count)
    chosen = jnp.where(filled_here, chosen, 0)
    return spread_rows(incoming, chosen, filled_here)


def cross_layer(
    samples_rows, key_rows, value_rows, text_limit, key_limit, w_query, w_out, first_row
):
    slot_count, row_count, feature_count = samples_rows.shape
    head_count = w_query.shape[1] // HEAD_DIM
    normal = normalize(samples_rows).reshape(slot_count * row_count, feature_count)
    queries = (
        jnp.dot(normal, w_query, preferred_element_type=jnp.float32) * HEAD_DIM ** (-0.5)
    ).astype(jnp.bfloat16)
    queries = queries.reshape(slot_count, row_count, head_count, HEAD_DIM)
    running_max = jnp.full((slot_count, head_count, row_count), masked_score, jnp.float32)
    piece_keys = lax.all_gather(key_rows, "seq", axis=1, tiled=True)
    piece_values = lax.all_gather(value_rows, "seq", axis=1, tiled=True)
    key_count = piece_keys.shape[1]
    head_keys = piece_keys.reshape(slot_count, key_count, head_count, HEAD_DIM)
    head_values = piece_values.reshape(slot_count, key_count, head_count, HEAD_DIM)
    scores = jnp.einsum("sqhd,skhd->shqk", queries, head_keys, preferred_element_type=jnp.float32)
    position = jnp.arange(key_count, dtype=jnp.int32)
    allowed = (position[None, :] < key_limit[:, None])[:, None, None, :]
    scores = jnp.where(allowed, scores, masked_score)
    new_max = jnp.maximum(running_max, jnp.max(scores, axis=-1))
    probs = jnp.where(allowed, jnp.exp(scores - new_max[..., None]), 0.0)
    running_sum = jnp.sum(probs, axis=-1)
    weights = probs.astype(jnp.bfloat16)
    running_ctx = jnp.einsum(
        "shqk,skhd->shqd", weights, head_values, preferred_element_type=jnp.float32
    )
    running_max, running_sum, running_ctx = (new_max, running_sum, running_ctx)
    context = running_ctx / running_sum[..., None]
    context = (
        context.transpose(0, 2, 1, 3)
        .reshape(slot_count * row_count, head_count * HEAD_DIM)
        .astype(jnp.bfloat16)
    )
    projected = jnp.dot(context, w_out, preferred_element_type=jnp.float32).reshape(
        slot_count, row_count, feature_count
    )
    row_position = first_row + jnp.arange(row_count, dtype=jnp.int32)
    kept_rows = row_position[None, :] < text_limit[:, None]
    return jnp.where(kept_rows[..., None], projected, 0.0).astype(jnp.bfloat16)


def on_device(
    tokens,
    image_keys,
    image_values,
    text_len,
    image_len,
    counts,
    old_group,
    new_group,
    w_query,
    w_out,
):
    group_count = lax.axis_size("group")
    slot_count = tokens.shape[0]
    row_count = tokens.shape[1]
    group_index = lax.axis_index("group")
    first_row = lax.axis_index("seq") * row_count
    tables = layout(counts, old_group, new_group, group_count, slot_count)
    own_first = group_index * slot_count
    text_limit = lax.dynamic_slice_in_dim(text_len, own_first, slot_count)
    key_limit = lax.dynamic_slice_in_dim(image_len, own_first, slot_count)
    attended = cross_layer(
        tokens, image_keys, image_values, text_limit, key_limit, w_query, w_out, first_row
    )
    return regroup(
        attended, group_index, group_count, slot_count, tables, counts, old_group, new_group
    )


def solution(mesh):
    in_specs = (
        P("group", "seq", None),
        P("group", "seq", None),
        P("group", "seq", None),
        P(),
        P(),
        P(),
        P(),
        P(),
        P(),
        P(),
    )
    out_specs = P("group", "seq", None)
    return jax.shard_map(
        on_device, mesh=mesh, in_specs=in_specs, out_specs=out_specs, check_vma=False
    )
```

profile of v0, /device:TPU:0, one launch (start us, length us, event | category | flops | bytes accessed | tf_op | source)
XLA Modules:
  0.0 466.5 jit_solution(17421429270864026179)
XLA Ops:
  6.5 2.9 copy.28
  9.5 0.7 all-gather.5.cloned.1.call-update
  10.2 4.7 %convert_reduce_fusion = f32[8,256]{1,0:T(8,128)S(1)} fusion(bf16[8,256,2048]{2,1,0:T(8,128)(2,1)} %param.10), kind=kLoop, calls=%fused_computation.7 | loop fusion | flops 8386560 | bytes 8396800 | tf_op jit(solution)/shard_map/reduce_sum | solution.py:36
  14.9 1.1 copy-done
  16.0 2.4 fusion.4
  18.3 2.5 fusion.5
  21.0 19.4 %fusion.21 = bf16[256,8,16,128]{3,1,2,0:T(8,128)(2,1)} fusion(bf16[2048,2048]{1,0:T(8,128)(2,1)S(1)} %bitcast.27, bf16[2048,2048]{1,0:T(8,128)(2,1)S(1)} %bitcast.31), kind=kOutput, calls=%fused_computation.27 | convolution fusion | flops 17188257792 | bytes 25165824 | tf_op jit(solution)/shard_map/dot_general | solution.py:73
  40.3 9.8 %copy.38 = bf16[256,8,16,128]{3,2,1,0:T(8,128)(2,1)} copy(bf16[256,8,16,128]{3,1,2,0:T(8,128)(2,1)} %fusion.21) | data formatting | bytes 16777216
  50.1 0.1 dynamic_slice.19
  50.2 0.1 dynamic_slice.18
  50.3 0.2 select_reduce_fusion.4
  50.5 0.2 select_reduce_fusion.6
  50.7 0.1 iota_add_fusion
  50.8 0.1 select_n.139
  50.8 0.1 add.104
  51.0 0.1 lt.144
  51.3 43.1 %all-gather.3.cloned.1.call-done = bf16[8,256,2048]{2,0,1:T(8,128)(2,1)} async-done(((bf16[8,32,2048]{2,0,1:T(8,128)(2,1)}), bf16[8,256,2048]{2,0,1:T(8,128)(2,1)}) %all-gather.3.cloned.1.call-update) | async-done | bytes 8388624 | tf_op jit(solution)/shard_map/all_gather | solution.py:77
  94.3 13.0 %copy.29 = bf16[8,256,2048]{1,2,0:T(8,128)(2,1)} copy(bf16[8,256,2048]{2,0,1:T(8,128)(2,1)} %all-gather.3.cloned.1.call-done) | data formatting | bytes 16777216 | tf_op jit(solution)/shard_map/all_gather | solution.py:77
  107.3 21.7 %select_reduce_fusion = (f32[8,16,256]{2,1,0:T(8,128)S(1)}, f32[8,16,256,256]{2,3,1,0:T(8,128)}) fusion(pred[8,256]{1,0:T(8,128)(4,1)S(1)} %iota_compare_fusion, bf16[8,256,16,128]{1,3,2,0:T(8,128)(2,1)} %bitcast.26, bf16[8,256,16,128]{3,2,1,0:T(8,128)(2,1)} %bitcast.25), kind=kOutput, calls=%fused_computation.3 | convolution fusion | flops 2164228096 | bytes 50464768 | tf_op jit(solution)/shard_map/sqhd,skhd->shqk/dot_general | solution.py:82
  129.1 14.7 %fusion = f32[8,16,256]{2,1,0:T(8,128)S(1)} fusion(f32[8,16,256,256]{2,3,1,0:T(8,128)} %get-tuple-element.18, f32[8,16,256]{2,1,0:T(8,128)S(1)} %broadcast_maximum_fusion, pred[8,256]{1,0:T(8,128)(4,1)S(1)} %iota_compare_fusion), kind=kLoop, calls=%fused_computation.4 | loop fusion | flops 33521664 | bytes 33818624 | tf_op jit(solution)/shard_map/reduce_sum | solution.py:88
  143.8 32.7 %all-gather.5.cloned.1.call-done = bf16[8,256,2048]{2,1,0:T(8,128)(2,1)} async-done(((bf16[8,32,2048]{2,1,0:T(8,128)(2,1)}), bf16[8,256,2048]{2,1,0:T(8,128)(2,1)}) %all-gather.5.cloned.1.call-update) | async-done | bytes 8388624 | tf_op jit(solution)/shard_map/all_gather | solution.py:78
  176.5 11.3 %copy.32 = bf16[8,256,2048]{1,2,0:T(8,128)(2,1)} copy(bf16[8,256,2048]{2,1,0:T(8,128)(2,1)} %all-gather.5.cloned.1.call-done) | data formatting | bytes 16777216 | tf_op jit(solution)/shard_map/all_gather | solution.py:78
  187.8 17.3 %fusion.8 = bf16[8,256,16,128]{1,3,2,0:T(8,128)(2,1)S(1)} fusion(f32[8,256,16]{1,2,0:T(8,128)S(1)} %bitcast.29, bf16[8,256,16,128]{1,3,2,0:T(8,128)(2,1)} %bitcast.28, f32[8,16,256,256]{2,3,1,0:T(8,128)} %get-tuple-element.18, f32[8,16,256]{2,1,0:T(8,128)S(1)} %broadcast_maximum_fusion, pred[8,256]{1,0:T(8,128)(4,1)S(1)} %iota_compare_fusion), kind=kOutput, calls=%fused_computation.14 | convolution fusion | flops 2189426688 | bytes 50595840 | tf_op jit(solution)/shard_map/shqk,skhd->shqd/dot_general | solution.py:90
  205.1 21.7 %select_convert_fusion = bf16[8,256,2048]{2,1,0:T(8,128)(2,1)} fusion(pred[8,256]{1,0:T(8,128)(4,1)S(1)} %broadcast_compare_fusion, bf16[8,256,2048]{1,2,0:T(8,128)(2,1)S(1)} %bitcast.32, bf16[2048,2048]{1,0:T(8,128)(2,1)} %param.19), kind=kOutput, calls=%fused_computation.16 | convolution fusion | flops 17188257792 | bytes 25167872 | tf_op jit(solution)/shard_map/dot_general | solution.py:100
  226.8 10.3 %gather_fusion = bf16[16,256,2048]{2,1,0:T(8,128)(2,1)} fusion(bf16[8,256,2048]{2,1,0:T(8,128)(2,1)} %select_convert_fusion, s32[1024]{0:T(1024)S(1)} %pad_clamp_fusion.1), kind=kCustom, calls=%fused_computation | custom fusion | bytes 33554496 | tf_op jit(solution)/shard_map/jit(_take)/gather | solution.py:43
  237.1 14.3 %select_select_fusion = bf16[16,256,2048]{2,1,0:T(8,128)(2,1)} fusion(bf16[16,256,2048]{2,1,0:T(8,128)(2,1)} %gather_fusion, pred[16]{0:T(512)(128)(4,1)S(1)} %compare_and_fusion.1, pred[16]{0:T(512)(128)(4,1)S(1)} %lt.144), kind=kLoop, calls=%fused_computation.15 | loop fusion | flops 16777216 | bytes 33554464 | tf_op jit(solution)/shard_map/jit(_where)/select_n | solution.py:44
  251.4 7.0 %all-to-all-start = ((bf16[16,256,2048]{2,1,0:T(8,128)(2,1)}), bf16[16,256,2048]{2,1,0:T(8,128)(2,1)}, u32[]{:S(2)}, u32[]{:S(2)}) async-start(bf16[16,256,2048]{2,1,0:T(8,128)(2,1)} %select_select_fusion), calls=%async_computation | async-start | bytes 33554432 | tf_op jit(solution)/shard_map/all_to_all | solution.py:60
  258.4 0.1 select_reduce_fusion.3
  258.5 0.1 compare_and_fusion.2
  258.6 182.7 %all-to-all-done = bf16[16,256,2048]{2,1,0:T(8,128)(2,1)} async-done(((bf16[16,256,2048]{2,1,0:T(8,128)(2,1)}), bf16[16,256,2048]{2,1,0:T(8,128)(2,1)}, u32[]{:S(2)}, u32[]{:S(2)}) %all-to-all-start) | async-done | bytes 16777248 | tf_op jit(solution)/shard_map/all_to_all | solution.py:60
  441.3 10.6 %gather_fusion.1 = bf16[8,256,2048]{2,1,0:T(8,128)(2,1)} fusion(bf16[16,256,2048]{2,1,0:T(8,128)(2,1)} %all-to-all-done, s32[1024]{0:T(1024)S(1)} %pad_clamp_fusion), kind=kCustom, calls=%fused_computation.1 | custom fusion | bytes 16777248 | tf_op jit(solution)/shard_map/jit(_take)/gather | solution.py:43
  451.9 7.7 %select_select_fusion.1 = bf16[8,256,2048]{2,1,0:T(8,128)(2,1)} fusion(bf16[8,256,2048]{2,1,0:T(8,128)(2,1)} %gather_fusion.1, pred[8]{0:T(512)(128)(4,1)S(1)} %get-tuple-element.11, pred[8]{0:T(512)(128)(4,1)S(1)} %get-tuple-element.13), kind=kLoop, calls=%fused_computation.26 | loop fusion | flops 8388608 | bytes 16777232 | tf_op jit(solution)/shard_map/jit(_where)/select_n | solution.py:44
  (35 shorter events, 0.5 us)
Async XLA Ops:
  6.5 87.8 %all-gather.3.cloned.1.call-start = ((), (), s32[]{:S(2)}) async-start(), calls=%async_computation.1 | async-start | bytes 9437184 | tf_op jit(solution)/shard_map/all_gather | solution.py:77
  9.4 167.1 %all-gather.5.cloned.1.call-start = ((), (), s32[]{:S(2)}) async-start(), calls=%async_computation.2 | async-start | bytes 9437184 | tf_op jit(solution)/shard_map/all_gather | solution.py:78
  10.2 5.8 %copy-start = (bf16[8,256,2048]{2,1,0:T(8,128)(2,1)S(1)}, bf16[8,256,2048]{2,1,0:T(8,128)(2,1)}, u32[]{:S(2)}) copy-start(bf16[8,256,2048]{2,1,0:T(8,128)(2,1)} %param.10) | copy-start | bytes 25165828
  16.0 4.9 %slice-start = ((s8[8388608]{0:T(1024)(128)(4,1)}), s8[4194304]{0:T(1024)(128)(4,1)S(1)}, s32[]{:S(2)}) async-start(s8[8388608]{0:T(1024)(128)(4,1)} %bitcast.30), calls=%async_computation.3 | async-start | bytes 8388608
  18.3 2.6 slice-start.1
  40.3 9.8 %copy-start.4 = (s32[32]{0:T(128)S(1)}, s32[32]{0:T(128)}, u32[]{:S(2)}) copy-start(s32[32]{0:T(128)} %param.14) | copy-start | bytes 388
  40.3 9.9 %copy-start.5 = (s32[32]{0:T(128)S(1)}, s32[32]{0:T(128)}, u32[]{:S(2)}) copy-start(s32[32]{0:T(128)} %param.13) | copy-start | bytes 388
  40.3 10.0 %copy-start.1 = (s32[6]{0:T(128)S(1)}, s32[6]{0:T(128)}, u32[]{:S(2)}) copy-start(s32[6]{0:T(128)} %param.17) | copy-start | bytes 76
  40.3 10.0 %copy-start.2 = (s32[6]{0:T(128)S(1)}, s32[6]{0:T(128)}, u32[]{:S(2)}) copy-start(s32[6]{0:T(128)} %param.16) | copy-start | bytes 76
  40.3 10.0 %copy-start.3 = (s32[6]{0:T(128)S(1)}, s32[6]{0:T(128)}, u32[]{:S(2)}) copy-start(s32[6]{0:T(128)} %param.15) | copy-start | bytes 76
  251.4 189.9 %all-to-all-start = ((bf16[16,256,2048]{2,1,0:T(8,128)(2,1)}), bf16[16,256,2048]{2,1,0:T(8,128)(2,1)}, u32[]{:S(2)}, u32[]{:S(2)}) async-start(bf16[16,256,2048]{2,1,0:T(8,128)(2,1)} %select_select_fusion), calls=%async_computation | async-start | bytes 33554432 | tf_op jit(solution)/shard_map/all_to_all | solution.py:60
Sparse Core Ops, SparseCore 0:
  9.6 84.7 all-gather.2
  95.9 80.5 all-gather.4
where the time goes:
time: 468 us; the launch traced here: 466 us
  waiting for transfers between devices  259 us (55%)
  matrix products  80.1 us (17%)
  local copies, waits for them, and re-layouts  59.4 us (13%)
  other arithmetic  47.2 us (10%)
  between operations  13.6 us (3%)
  starting transfers between devices  7 us (1%)
    all_to_all x1, waiting for transfers between devices, regroup(): lax.all_to_all(outgoing, 'group', split_axis=0, concat_axis=0, tiled=True)  183 us
    all_gather x1, waiting for transfers between devices, cross_layer(): piece_keys = lax.all_gather(key_rows, 'seq', axis=1, tiled=True)  43.1 us
    all_gather x1, waiting for transfers between devices, cross_layer(): piece_values = lax.all_gather(value_rows, 'seq', axis=1, tiled=True)  32.7 us
    select_n x2, other arithmetic, spread_rows(): jnp.where(wanted[:, None, None], gathered, jnp.zeros((), source_array.dty...  22 us
    dot_general x1, matrix products, cross_layer(): jnp.einsum('sqhd,skhd->shqk', queries, head_keys, preferred_element_type=...  21.7 us
    dot_general x1, matrix products, cross_layer(): jnp.dot(context, w_out, preferred_element_type=jnp.float32)  21.7 us
    gather x2, local copies, waits for them, and re-layouts, spread_rows(): gathered = jnp.take(source_array, source_index, axis=0)  20.9 us
    dot_general x1, matrix products, cross_layer(): jnp.dot(normal, w_query, preferred_element_type=jnp.float32)  19.4 us
  transfers between devices with their start and end apart: 3, of which 3 were waited for; matrix products, arithmetic and copies ran while one was open for 19% of the time, Pallas kernels for 0%

commit v1 on v0

--- a/solution.py
+++ b/solution.py
@@ -74,8 +74,11 @@
     ).astype(jnp.bfloat16)
     queries = queries.reshape(slot_count, row_count, head_count, HEAD_DIM)
     running_max = jnp.full((slot_count, head_count, row_count), masked_score, jnp.float32)
-    piece_keys = lax.all_gather(key_rows, "seq", axis=1, tiled=True)
-    piece_values = lax.all_gather(value_rows, "seq", axis=1, tiled=True)
+    piece_keys, piece_values = jnp.split(
+        lax.all_gather(jnp.concatenate([key_rows, value_rows], axis=0), "seq", axis=1, tiled=True),
+        [key_rows.shape[0]],
+        axis=0,
+    )
     key_count = piece_keys.shape[1]
     head_keys = piece_keys.reshape(slot_count, key_count, head_count, HEAD_DIM)
     head_values = piece_values.reshape(slot_count, key_count, head_count, HEAD_DIM)

time: 468 us -> 520 us (1.11)
  waiting for transfers between devices: 259 us -> 293 us
  local copies, waits for them, and re-layouts: 59.4 us -> 72 us
  other arithmetic: 47.2 us -> 52.7 us
    all_gather x2 -> x1, waiting for transfers between devices: 75.8 us -> 110 us  [cross_layer(): lax.all_gather(jnp.concatenate([key_rows, value_rows], axis=0), 'seq', ax...]
    split x0 -> x2, local copies, waits for them, and re-layouts: none -> 24.9 us  [cross_layer(): jnp.split(lax.all_gather(jnp.concatenate([key_rows, value_rows], axis=0),...]
    all_gather x2 -> x0, local copies, waits for them, and re-layouts: 24.3 us -> none  [the longest x1 13 us: cross_layer(): piece_keys = lax.all_gather(key_rows, 'seq', axis=1, tiled=True)]
    unnamed x18 -> x22, local copies, waits for them, and re-layouts: 13.8 us -> 23.2 us
  transfers between devices with their start and end apart: 3 -> 2, of which waited for: 3 -> 2; matrix products, arithmetic and copies ran while one was open for 19% -> 8% of each run, Pallas kernels for 0% -> 0%
where the time goes in v1:
time: 520 us; the launch traced here: 519 us
  waiting for transfers between devices  293 us (56%)
  matrix products  81.2 us (16%)
  local copies, waits for them, and re-layouts  72 us (14%)
  other arithmetic  52.7 us (10%)
  between operations  13.6 us (3%)
  starting transfers between devices  6.96 us (1%)
    all_to_all x1, waiting for transfers between devices, regroup(): lax.all_to_all(outgoing, 'group', split_axis=0, concat_axis=0, tiled=True)  183 us
    all_gather x1, waiting for transfers between devices, cross_layer(): lax.all_gather(jnp.concatenate([key_rows, value_rows], axis=0), 'seq', ax...  110 us
    split x2, local copies, waits for them, and re-layouts, cross_layer(): jnp.split(lax.all_gather(jnp.concatenate([key_rows, value_rows], axis=0),...  24.9 us
    dot_general x1, matrix products, cross_layer(): jnp.dot(context, w_out, preferred_element_type=jnp.float32)  23.7 us
    unnamed x22, local copies, waits for them, and re-layouts  23.2 us
    select_n x2, other arithmetic, spread_rows(): jnp.where(wanted[:, None, None], gathered, jnp.zeros((), source_array.dty...  22 us
    dot_general x1, matrix products, cross_layer(): jnp.einsum('sqhd,skhd->shqk', queries, head_keys, preferred_element_type=...  21.7 us
    gather x2, local copies, waits for them, and re-layouts, spread_rows(): gathered = jnp.take(source_array, source_index, axis=0)  20.9 us
  transfers between devices with their start and end apart: 2, of which 2 were waited for; matrix products, arithmetic and copies ran while one was open for 8% of the time, Pallas kernels for 0%

profile of v1, /device:TPU:0, one launch (start us, length us, event | category | flops | bytes accessed | tf_op | source)
XLA Modules:
  0.0 519.1 jit_solution(6655881202671598754)
XLA Ops:
  6.5 1.7 pad_maximum_fusion
  8.3 2.5 copy.28
  10.8 4.7 convert_reduce_fusion
  15.5 5.9 %fusion.4 = f32[8,256]{1,0:T(8,128)S(1)} fusion(bf16[8,256,2048]{2,1,0:T(8,128)(2,1)} %param.10, f32[8,256]{1,0:T(8,128)S(1)} %broadcast_multiply_fusion), kind=kLoop, calls=%fused_computation.10 | loop fusion | flops 16775168 | bytes 8404992 | tf_op jit(solution)/shard_map/reduce_sum | solution.py:38
  21.5 2.5 fusion.5
  24.0 0.4 slice-done.3
  24.4 19.4 %fusion.21 = bf16[256,8,16,128]{3,1,2,0:T(8,128)(2,1)} fusion(bf16[2048,2048]{1,0:T(8,128)(2,1)S(1)} %bitcast.29, bf16[2048,2048]{1,0:T(8,128)(2,1)S(1)} %bitcast.33), kind=kOutput, calls=%fused_computation.27 | convolution fusion | flops 17188257792 | bytes 25165824 | tf_op jit(solution)/shard_map/dot_general | solution.py:73
  43.8 9.9 %copy.39 = bf16[256,8,16,128]{3,2,1,0:T(8,128)(2,1)} copy(bf16[256,8,16,128]{3,1,2,0:T(8,128)(2,1)} %fusion.21) | data formatting | bytes 16777216
  53.7 0.1 dynamic_slice.19
  53.8 0.1 dynamic_slice.18
  53.9 0.2 select_reduce_fusion.4
  54.1 0.2 select_reduce_fusion.6
  54.2 0.1 iota_add_fusion
  54.3 0.1 select_n.139
  54.4 0.1 add.104
  54.6 0.1 lt.144
  54.8 109.9 %all-gather.2.cloned.1.call-done = bf16[16,256,2048]{2,0,1:T(8,128)(2,1)} async-done(((bf16[16,32,2048]{2,0,1:T(8,128)(2,1)}), bf16[16,256,2048]{2,0,1:T(8,128)(2,1)}) %all-gather.2.cloned.1.call-update) | async-done | bytes 16777232 | tf_op jit(solution)/shard_map/all_gather | solution.py:78
  164.8 12.0 %fusion.29 = (bf16[8,256,2048]{2,0,1:T(8,128)(2,1)}, bf16[8,256,2048]{2,0,1:T(8,128)(2,1)}) fusion(bf16[16,256,2048]{2,0,1:T(8,128)(2,1)} %all-gather.2.cloned.1.call-done), kind=kLoop, calls=%fused_computation.67 | loop fusion | bytes 33554432 | tf_op jit(solution)/shard_map/split | solution.py:77
  176.7 12.9 %copy.38 = bf16[8,256,2048]{1,2,0:T(8,128)(2,1)} copy(bf16[8,256,2048]{2,0,1:T(8,128)(2,1)} %get-tuple-element.16) | data formatting | bytes 16777216
  189.6 21.7 %select_reduce_fusion = (f32[8,16,256]{2,1,0:T(8,128)S(1)}, f32[8,16,256,256]{2,3,1,0:T(8,128)}) fusion(pred[8,256]{1,0:T(8,128)(4,1)S(1)} %iota_compare_fusion, bf16[8,256,16,128]{1,3,2,0:T(8,128)(2,1)} %bitcast.28, bf16[8,256,16,128]{3,2,1,0:T(8,128)(2,1)} %bitcast.27), kind=kOutput, calls=%fused_computation.3 | convolution fusion | flops 2164228096 | bytes 50464768 | tf_op jit(solution)/shard_map/sqhd,skhd->shqk/dot_general | solution.py:85
  211.3 12.9 %copy.32 = bf16[8,256,2048]{1,2,0:T(8,128)(2,1)} copy(bf16[8,256,2048]{2,0,1:T(8,128)(2,1)} %get-tuple-element.15) | data formatting | bytes 16777216 | tf_op jit(solution)/shard_map/split | solution.py:77
  224.2 15.0 %fusion = f32[8,16,256]{2,1,0:T(8,128)S(1)} fusion(f32[8,16,256,256]{2,3,1,0:T(8,128)} %get-tuple-element.20, f32[8,16,256]{2,1,0:T(8,128)S(1)} %broadcast_maximum_fusion, pred[8,256]{1,0:T(8,128)(4,1)S(1)} %iota_compare_fusion), kind=kLoop, calls=%fused_computation.4 | loop fusion | flops 33521664 | bytes 33818624 | tf_op jit(solution)/shard_map/reduce_sum | solution.py:91
  239.2 16.5 %fusion.8 = bf16[8,256,16,128]{1,3,2,0:T(8,128)(2,1)} fusion(f32[8,256,16]{1,2,0:T(8,128)S(1)} %bitcast.31, bf16[8,256,16,128]{1,3,2,0:T(8,128)(2,1)S(1)} %bitcast.30, f32[8,16,256,256]{2,3,1,0:T(8,128)} %get-tuple-element.20, f32[8,16,256]{2,1,0:T(8,128)S(1)} %broadcast_maximum_fusion, pred[8,256]{1,0:T(8,128)(4,1)S(1)} %iota_compare_fusion), kind=kOutput, calls=%fused_computation.14 | convolution fusion | flops 2189426688 | bytes 50595840 | tf_op jit(solution)/shard_map/shqk,skhd->shqd/dot_general | solution.py:93
  255.7 23.7 %select_convert_fusion = bf16[8,256,2048]{2,1,0:T(8,128)(2,1)} fusion(pred[8,256]{1,0:T(8,128)(4,1)S(1)} %broadcast_compare_fusion, bf16[8,256,2048]{1,2,0:T(8,128)(2,1)} %bitcast.34, bf16[2048,2048]{1,0:T(8,128)(2,1)} %param.19), kind=kOutput, calls=%fused_computation.16 | convolution fusion | flops 17188257792 | bytes 25167872 | tf_op jit(solution)/shard_map/dot_general | solution.py:103
  279.4 10.3 %gather_fusion = bf16[16,256,2048]{2,1,0:T(8,128)(2,1)} fusion(bf16[8,256,2048]{2,1,0:T(8,128)(2,1)} %select_convert_fusion, s32[1024]{0:T(1024)S(1)} %pad_clamp_fusion.1), kind=kCustom, calls=%fused_computation | custom fusion | bytes 33554496 | tf_op jit(solution)/shard_map/jit(_take)/gather | solution.py:43
  289.7 14.3 %select_select_fusion = bf16[16,256,2048]{2,1,0:T(8,128)(2,1)} fusion(bf16[16,256,2048]{2,1,0:T(8,128)(2,1)} %gather_fusion, pred[16]{0:T(512)(128)(4,1)S(1)} %compare_and_fusion.1, pred[16]{0:T(512)(128)(4,1)S(1)} %lt.144), kind=kLoop, calls=%fused_computation.15 | loop fusion | flops 16777216 | bytes 33554464 | tf_op jit(solution)/shard_map/jit(_where)/select_n | solution.py:44
  304.0 7.0 %all-to-all-start = ((bf16[16,256,2048]{2,1,0:T(8,128)(2,1)}), bf16[16,256,2048]{2,1,0:T(8,128)(2,1)}, u32[]{:S(2)}, u32[]{:S(2)}) async-start(bf16[16,256,2048]{2,1,0:T(8,128)(2,1)} %select_select_fusion), calls=%async_computation | async-start | bytes 33554432 | tf_op jit(solution)/shard_map/all_to_all | solution.py:60
  311.0 0.1 select_reduce_fusion.3
  311.1 0.1 compare_and_fusion.2
  311.2 182.7 %all-to-all-done = bf16[16,256,2048]{2,1,0:T(8,128)(2,1)} async-done(((bf16[16,256,2048]{2,1,0:T(8,128)(2,1)}), bf16[16,256,2048]{2,1,0:T(8,128)(2,1)}, u32[]{:S(2)}, u32[]{:S(2)}) %all-to-all-start) | async-done | bytes 16777248 | tf_op jit(solution)/shard_map/all_to_all | solution.py:60
  493.9 10.6 %gather_fusion.1 = bf16[8,256,2048]{2,1,0:T(8,128)(2,1)} fusion(bf16[16,256,2048]{2,1,0:T(8,128)(2,1)} %all-to-all-done, s32[1024]{0:T(1024)S(1)} %pad_clamp_fusion), kind=kCustom, calls=%fused_computation.1 | custom fusion | bytes 16777248 | tf_op jit(solution)/shard_map/jit(_take)/gather | solution.py:43
  504.5 7.7 %select_select_fusion.1 = bf16[8,256,2048]{2,1,0:T(8,128)(2,1)} fusion(bf16[8,256,2048]{2,1,0:T(8,128)(2,1)} %gather_fusion.1, pred[8]{0:T(512)(128)(4,1)S(1)} %get-tuple-element.11, pred[8]{0:T(512)(128)(4,1)S(1)} %get-tuple-element.13), kind=kLoop, calls=%fused_computation.26 | loop fusion | flops 8388608 | bytes 16777232 | tf_op jit(solution)/shard_map/jit(_where)/select_n | solution.py:44
  (39 shorter events, 0.4 us)
Async XLA Ops:
  6.5 158.2 %all-gather.2.cloned.1.call-start = ((), (), s32[]{:S(2)}) async-start(), calls=%async_computation.1 | async-start | bytes 18874368 | tf_op jit(solution)/shard_map/all_gather | solution.py:78
  10.8 10.6 %slice-start = ((s8[8388608]{0:T(1024)(128)(4,1)}), s8[4194304]{0:T(1024)(128)(4,1)S(1)}, s32[]{:S(2)}) async-start(s8[8388608]{0:T(1024)(128)(4,1)} %bitcast.25), calls=%async_computation.2 | async-start | bytes 8388608
  15.5 5.9 %slice-start.1 = ((s8[8388608]{0:T(1024)(128)(4,1)}), s8[4194304]{0:T(1024)(128)(4,1)S(1)}, s32[]{:S(2)}) async-start(s8[8388608]{0:T(1024)(128)(4,1)} %bitcast.25), calls=%async_computation.3 | async-start | bytes 8388608
  15.5 8.5 %slice-start.2 = ((s8[8388608]{0:T(1024)(128)(4,1)}), s8[4194304]{0:T(1024)(128)(4,1)S(1)}, s32[]{:S(2)}) async-start(s8[8388608]{0:T(1024)(128)(4,1)} %bitcast.32), calls=%async_computation.4 | async-start | bytes 8388608
  21.5 3.0 slice-start.3
  43.8 9.9 %copy-start.4 = (s32[32]{0:T(128)S(1)}, s32[32]{0:T(128)}, u32[]{:S(2)}) copy-start(s32[32]{0:T(128)} %param.14) | copy-start | bytes 388
  43.8 10.0 %copy-start.5 = (s32[32]{0:T(128)S(1)}, s32[32]{0:T(128)}, u32[]{:S(2)}) copy-start(s32[32]{0:T(128)} %param.13) | copy-start | bytes 388
  43.8 10.1 %copy-start.1 = (s32[6]{0:T(128)S(1)}, s32[6]{0:T(128)}, u32[]{:S(2)}) copy-start(s32[6]{0:T(128)} %param.17) | copy-start | bytes 76
  43.8 10.1 %copy-start.2 = (s32[6]{0:T(128)S(1)}, s32[6]{0:T(128)}, u32[]{:S(2)}) copy-start(s32[6]{0:T(128)} %param.16) | copy-start | bytes 76
  43.8 10.1 %copy-start.3 = (s32[6]{0:T(128)S(1)}, s32[6]{0:T(128)}, u32[]{:S(2)}) copy-start(s32[6]{0:T(128)} %param.15) | copy-start | bytes 76
  224.2 15.0 %copy-start = (bf16[8,256,2048]{1,2,0:T(8,128)(2,1)S(1)}, bf16[8,256,2048]{1,2,0:T(8,128)(2,1)}, u32[]{:S(2)}) copy-start(bf16[8,256,2048]{1,2,0:T(8,128)(2,1)} %copy.32) | copy-start | bytes 25165828
  304.0 189.9 %all-to-all-start = ((bf16[16,256,2048]{2,1,0:T(8,128)(2,1)}), bf16[16,256,2048]{2,1,0:T(8,128)(2,1)}, u32[]{:S(2)}, u32[]{:S(2)}) async-start(bf16[16,256,2048]{2,1,0:T(8,128)(2,1)} %select_select_fusion), calls=%async_computation | async-start | bytes 33554432 | tf_op jit(solution)/shard_map/all_to_all | solution.py:60
Sparse Core Ops, SparseCore 0:
  10.9 153.7 all-gather.1
